TPU v7x, 256 devices: a whole 4x4x8 slice. The times are simulated.
256 devices in a mesh: pack: 32 (over y, z), hist: 8 (over x, core).
Axes of the slice: x: 4, y: 4, z: 8, core: 2. Of those that a mesh axis runs over, the one named last changes fastest.
Arguments:
- queries: bfloat16 [32, 4096, 2048], P('pack', 'hist'), may hold values from -0.59765625 to 0.59765625
- keys: bfloat16 [32, 4096, 2048], P('pack', 'hist'), may hold values from -6 to 6
- values: bfloat16 [32, 4096, 2048], P('pack', 'hist'), may hold values from -6 to 6
- gates: bfloat16 [32, 4096, 2048], P('pack', 'hist'), may hold values from -6 to 6
- user_ids: int32 [32, 4096], P('pack', 'hist'), may hold values from 0 to 5, never falling along the last dimension, each value on 1 to 1365 neighbouring positions
- forget_rate: float32 [16], replicated, may hold values from 0.0001 to 0.02
- norm_gain: float32 [2048], replicated, may hold values from 0.1 to 1.9
- w_out: bfloat16 [2048, 2048], P('pack'), may hold values from -0.125 to 0.125
Outputs:
- mixed: bfloat16 [32, 4096, 2048], P('pack', 'hist')
Inputs may be any that keep to these rules, and one draw needn't show every extreme that they name: `user_ids`: in each window user ids never fall along the events; each user holds 1 to 1365 consecutive events, and one user exactly 1365.
All inputs are finite; a program needn't handle non-finite values.
Results may differ from a plain program's by a relative error of at most 0.0061.
Values may be sent and summed in bfloat16 or wider, within the bound.
No kernel may reach another device: no remote copies, remote signals or barrier semaphores. Data moves between devices by JAX's collectives and lax.ppermute only.
A program may use at most 128 MiB of HBM per device.

v0:
```python
import jax
import jax.numpy as jnp
from jax import lax
from jax.sharding import PartitionSpec as P

HEADS = 16
GROUP = 128


def passed_along(array, axis, by):
    size = lax.axis_size(axis)
    pairs = [(i, i + by) for i in range(size) if 0 <= i + by < size]
    return lax.ppermute(array, axis, pairs)


def carried_in(array, axis, combine, identity):
    size, here = (lax.axis_size(axis), lax.axis_index(axis))
    everything = jax.tree.map(lambda part: lax.all_gather(part, axis), array)
    start = jax.tree.map(
        lambda part, zero: jnp.broadcast_to(jnp.asarray(zero, part.dtype), part.shape),
        array,
        identity,
    )

    def hop(k, before):
        reached = k < here
        new = combine(before, jax.tree.map(lambda part: part[k], everything))
        return jax.tree.map(lambda a, b: jnp.where(reached, a, b), new, before)

    return lax.fori_loop(0, size, hop, start)


def combine_states(earlier, later):
    return (earlier[0] * later[0], later[0][:, None, None] * earlier[1] + later[1])


def local(queries, keys, values, gates, user_ids, forget_rate, norm_gain, w_out):
    length = queries.shape[1]
    width = queries.shape[2]
    head_dim = width // HEADS
    blocks = length // GROUP
    log_decay = jnp.log1p(-forget_rate)
    users = user_ids[0]
    before = passed_along(users[length - 1 :], "hist", 1)
    prior = jnp.concatenate([before, users[:-1]])
    place_all = jnp.arange(length, dtype=jnp.int32)
    forced = jnp.logical_and(lax.axis_index("hist") == 0, place_all == 0)
    starts = jnp.logical_or(users != prior, forced).astype(jnp.int32)
    seg = users.reshape(blocks, GROUP)
    start_blk = starts.reshape(blocks, GROUP)
    q_blk = queries[0].reshape(blocks, GROUP, HEADS, head_dim)
    k_blk = keys[0].reshape(blocks, GROUP, HEADS, head_dim)
    v_blk = values[0].reshape(blocks, GROUP, HEADS, head_dim)
    place = jnp.arange(GROUP, dtype=jnp.int32)
    diff = place[:, None] - place[None, :]
    causal = diff >= 0
    lag = jnp.where(causal, diff, 0).astype(jnp.float32)
    decay = jnp.exp(lag[None] * log_decay[:, None, None])
    mask = jnp.logical_and(seg[:, :, None] == seg[:, None, :], causal[None])
    scores = jnp.einsum("nthd,nshd->nhts", q_blk, k_blk, preferred_element_type=jnp.float32)
    weights = jnp.where(mask[:, None], scores * decay[None], 0.0).astype(jnp.bfloat16)
    inner = jnp.einsum("nhts,nshd->nthd", weights, v_blk, preferred_element_type=jnp.float32)
    tail = jnp.exp((GROUP - 1 - place).astype(jnp.float32)[None, :] * log_decay[:, None])
    keep_rows = (seg == seg[:, -1:]).astype(jnp.float32)
    scaled = (k_blk * (keep_rows[:, :, None] * tail.T[None])[..., None]).astype(jnp.bfloat16)
    own = jnp.einsum("nshd,nshe->nhde", scaled, v_blk, preferred_element_type=jnp.float32)
    any_start = jnp.max(start_blk, axis=1) > 0
    keep = jnp.where(any_start[:, None], 0.0, jnp.exp(GROUP * log_decay)[None, :])

    def advance(state, item):
        keep_c, own_c = item
        return (keep_c[:, None, None] * state + own_c, state)

    zero_state = jnp.zeros((HEADS, head_dim, head_dim), jnp.float32)
    local_final, local_enter = lax.scan(advance, zero_state, (keep, own))
    keep_before = jnp.cumprod(
        jnp.concatenate([jnp.ones((1, HEADS), jnp.float32), keep[:-1]], axis=0), axis=0
    )
    keep_device = keep_before[-1] * keep[-1]
    identity = (
        jnp.ones((HEADS,), jnp.float32),
        jnp.zeros((HEADS, head_dim, head_dim), jnp.float32),
    )
    incoming = carried_in((keep_device, local_final), "hist", combine_states, identity)[1]
    entering = (local_enter + keep_before[:, :, None, None] * incoming[None]).astype(jnp.bfloat16)
    open_run = (jnp.cumsum(start_blk, axis=1) == 0).astype(jnp.float32)
    reach = jnp.exp((place + 1).astype(jnp.float32)[:, None] * log_decay[None, :])
    factor = open_run[:, :, None] * reach[None]
    carried = (
        jnp.einsum("nthd,nhde->nthe", q_blk, entering, preferred_element_type=jnp.float32)
        * factor[..., None]
    )
    retained = (inner + carried).reshape(length, HEADS, head_dim)
    mean = jnp.mean(retained, axis=2, keepdims=True)
    centred = retained - mean
    variance = jnp.mean(centred * centred, axis=2, keepdims=True)
    normed = (centred * lax.rsqrt(variance + 1e-05)).reshape(length, width) * norm_gain
    gated = (jax.nn.silu(gates[0].astype(jnp.float32)) * normed).astype(jnp.bfloat16)
    mixed = jnp.dot(
        gated, lax.all_gather(w_out, "pack", axis=0, tiled=True), preferred_element_type=jnp.float32
    ).astype(jnp.bfloat16)
    return mixed[None]


def solution(mesh):
    in_specs = (
        P("pack", "hist", None),
        P("pack", "hist", None),
        P("pack", "hist", None),
        P("pack", "hist", None),
        P("pack", "hist"),
        P(),
        P(),
        P("pack", None),
    )
    out_specs = P("pack", "hist", None)
    return jax.shard_map(local, mesh=mesh, in_specs=in_specs, out_specs=out_specs, check_vma=False)
```

profile of v0, /device:TPU:1, one launch (start us, length us, event | category | flops | bytes accessed | tf_op | source)
XLA Modules:
  0.0 219.2 jit_solution(17431535320970974348)
XLA Ops:
  6.5 1.2 slice.26
  7.8 4.5 %collective-permute-start = (s32[1]{0:T(128)}, s32[1]{0:T(128)}, u32[]{:S(2)}, u32[]{:S(2)}) collective-permute-start(s32[1]{0:T(128)} %bitcast.4), channel_id=1, source_target_pairs={{0,1},{1,2},{2,3},{3,4},{4,5},{5,6},{6,7},{8,9},{9,10},{10,11},{11... | collective-permute-start | bytes 20 | tf_op jit(solution)/shard_map/ppermute | solution.py:13
  12.3 0.9 slice_reduce_fusion
  13.2 0.8 compare_convert_fusion.1
  13.9 0.7 multiply_exponential_fusion.3
  14.6 3.5 %copy.41 = bf16[64,8,16,128]{3,2,1,0:T(8,128)(2,1)} copy(bf16[64,8,16,128]{3,1,2,0:T(8,128)(2,1)} %bitcast.105) | data formatting | bytes 4194304
  18.1 3.5 %copy.26 = bf16[4,128,16,128]{1,3,2,0:T(8,128)(2,1)S(1)} copy(bf16[4,128,16,128]{3,2,1,0:T(8,128)(2,1)} %bitcast.100) | data formatting | bytes 4194304 | tf_op jit(solution)/shard_map/reshape;squeeze | solution.py:52
  21.6 4.3 %copy.42 = bf16[64,8,16,128]{3,2,1,0:T(8,128)(2,1)} copy(bf16[64,8,16,128]{3,1,2,0:T(8,128)(2,1)} %bitcast.106) | data formatting | bytes 4194304
  25.9 0.1 multiply_exponential_fusion.1
  26.0 0.8 fusion.31
  26.8 0.3 reduce_window_sum.11
  27.2 4.3 %fusion.10 = f32[4,16,128,128]{3,2,1,0:T(8,128)} fusion(bf16[4,128,16,128]{1,3,2,0:T(8,128)(2,1)S(1)} %copy.26, f32[4,128,16]{1,2,0:T(8,128)S(1)} %get-tuple-element.195, bf16[4,128,16,128]{3,2,1,0:T(8,128)(2,1)} %bitcast.98), kind=kOutput, calls=%fused_computation.25 | convolution fusion | flops 271581184 | bytes 8421376 | tf_op jit(solution)/shard_map/nshd,nshe->nhde/dot_general | solution.py:66
  31.6 10.0 %while.29 = (s32[]{:T(128)}, f32[16,128,128]{2,1,0:T(8,128)S(1)}, f32[4,16,128,128]{3,2,1,0:T(8,128)}, f32[4,16]{1,0:T(4,128)S(1)}, f32[4,16,128,128]{3,2,1,0:T(8,128)}) while((s32[]{:T(128)}, f32[16,128,128]{2,1,0:T(8,128)S(1)}, f32[4,16,128,128]{3,2,1,0:T(8,128)}, f32[4,16]{1,0:T(4,128)S(1)}, ...), condition=%wide.region_2.3_spmd.clone.clone, body=%wide.region_1.2_spmd.clone.sunk.clone | while | flops 1048579 | bytes 5243664 | solution.py:75
  31.6 1.1 bitcast_dynamic-update-slice_fusion.3
  32.6 1.4 bitcast_add_fusion.4
  34.1 1.1 bitcast_dynamic-update-slice_fusion.3
  35.1 1.4 bitcast_add_fusion.4
  36.6 1.1 bitcast_dynamic-update-slice_fusion.3
  37.7 1.4 bitcast_add_fusion.4
  39.1 1.1 bitcast_dynamic-update-slice_fusion.3
  40.2 1.4 bitcast_add_fusion.4
  41.6 1.0 copy-done
  42.6 0.7 all-gather.5.cloned.1.call-update
  43.4 2.2 %copy.40 = bf16[64,8,16,128]{3,2,1,0:T(8,128)(2,1)S(1)} copy(bf16[64,8,16,128]{3,1,2,0:T(8,128)(2,1)} %bitcast.107) | data formatting | bytes 4194304
  45.6 0.1 compare_and_fusion
  45.8 1.2 multiply_exponential_fusion
  46.9 6.8 %fusion.17 = f32[4,16,128,128]{2,3,1,0:T(8,128)} fusion(bf16[4,128,16,128]{3,2,1,0:T(8,128)(2,1)} %bitcast.99, bf16[4,128,16,128]{1,3,2,0:T(8,128)(2,1)} %copy-done.1, f32[16,128,128]{2,1,0:T(8,128)} %multiply_exponential_fusion, pred[4,128,128]{2,1,0:T(8,128)(4,1)S(1)} %compare_and_fusion, bf16[4,128,16,128]{3,2,1,0:T(8,128)(2,1)S(1)} %bitcast.96), kind=kOutput, calls=%fused_computation.31 | convolution fusion | flops 540016640 | bytes 11599872 | tf_op jit(solution)/shard_map/nhts,nshd->nthd/dot_general | solution.py:62
  53.8 9.5 %all-gather.1 = f32[8,1,16]{2,1,0:T(1,128)S(1)} all-gather(f32[1,1,16]{2,1,0:T(1,128)S(1)} %multiply_bitcast_fusion), channel_id=1, replica_groups=mesh['pack'=32,'hist'=8] {'hist'}, dimensions={0}, use_global_device_ids=true | all-gather | bytes 576 | tf_op jit(solution)/shard_map/all_gather | solution.py:18
  63.3 34.2 %all-gather.7.cloned.1.call-done = f32[128,128,128]{2,1,0:T(8,128)} async-done(((f32[16,128,128]{2,1,0:T(8,128)}), f32[128,128,128]{2,1,0:T(8,128)}) %all-gather.7.cloned.1.call-update) | async-done | bytes 8388624 | tf_op jit(solution)/shard_map/all_gather | solution.py:18
  97.5 11.9 %while.30 = (s32[]{:T(128)}, f32[16,128,128]{2,1,0:T(8,128)S(1)}, s32[]{:T(128)}, f32[8,16]{1,0:T(8,128)S(1)}, f32[8,16,128,128]{3,2,1,0:T(8,128)}) while((s32[]{:T(128)}, f32[16,128,128]{2,1,0:T(8,128)S(1)}, s32[]{:T(128)}, f32[8,16]{1,0:T(8,128)S(1)}, f32[8,16,128,128]{3,2,1,0:T(8,128)}) %tuple.71), condition=%wide.region_5.6_spmd.clone.clone, body=%wide.region_4.5_spmd.clone.sunk.clone | while | flops 1048580 | bytes 3146009 | solution.py:30
  97.5 1.5 fusion.41
  99.0 1.5 fusion.41
  100.5 1.5 fusion.41
  102.0 1.5 fusion.41
  103.5 1.5 fusion.41
  105.0 1.5 fusion.41
  106.5 1.5 fusion.41
  108.0 1.5 fusion.41
  109.5 7.4 %fusion.33 = (f32[4,128,16]{1,2,0:T(8,128)S(1)}, f32[4,128,16,128]{1,3,2,0:T(8,128)}) fusion(f32[4,128,16]{1,2,0:T(8,128)S(1)} %get-tuple-element.194, bf16[4,128,16,128]{3,2,1,0:T(8,128)(2,1)S(1)} %bitcast.97, f32[4,16,128,128]{3,2,1,0:T(8,128)} %get-tuple-element.127, f32[16,128,128]{2,1,0:T(8,128)S(1)} %get-tuple-element.129, ...), kind=kOutput, calls=%fused_computation.66 | convolution fusion | flops 274718720 | bytes 15794432 | tf_op jit(solution)/shard_map/nthd,nhde->nthe/dot_general | solution.py:90
  116.9 0.1 copy.36
  117.0 5.4 %copy.30 = f32[4,128,16,128]{3,2,1,0:T(8,128)} copy(f32[4,128,16,128]{1,3,2,0:T(8,128)} %get-tuple-element.193) | data formatting | bytes 8388608 | tf_op jit(solution)/shard_map/add | solution.py:93
  122.4 3.0 %multiply_reduce_fusion = f32[4,128,16]{1,2,0:T(8,128)S(1)} fusion(f32[4,128,16,128]{1,3,2,0:T(8,128)} %get-tuple-element.193, f32[4,128,16]{1,2,0:T(8,128)S(1)} %broadcast_multiply_fusion), kind=kLoop, calls=%fused_computation.18 | loop fusion | flops 3137536 | bytes 4259840 | tf_op jit(solution)/shard_map/reduce_sum | solution.py:96
  125.5 0.1 copy.37
  125.6 71.4 %all-gather.5.cloned.1.call-done = bf16[2048,2048]{1,0:T(8,128)(2,1)} async-done(((bf16[64,2048]{1,0:T(8,128)(2,1)}), bf16[2048,2048]{1,0:T(8,128)(2,1)}) %all-gather.5.cloned.1.call-update) | async-done | bytes 8388624 | tf_op jit(solution)/shard_map/all_gather | solution.py:100
  197.1 1.1 mul.221
  198.2 1.1 sub.57
  199.4 0.6 copy-done.4
  199.9 12.4 %fusion.9 = bf16[1,512,2048]{2,1,0:T(8,128)(2,1)} fusion(bf16[2048,2048]{1,0:T(8,128)(2,1)} %all-gather.5.cloned.1.call-done, f32[64,8,16,128]{3,2,1,0:T(8,128)S(1)} %bitcast.102, f32[64,8,16,128]{3,2,1,0:T(8,128)S(1)} %bitcast.103, f32[64,8,16,128]{3,2,1,0:T(8,128)S(1)} %bitcast.101, bf16[1,512,2048]{2,1,0:T(8,128)(2,1)S(1)} %copy-done.4, ...), kind=kOutput, calls=%fused_computation.24 | convolution fusion | flops 4306501632 | bytes 25174016 | tf_op jit(solution)/shard_map/dot_general | solution.py:99
  (41 shorter events, 0.4 us)
Async XLA Ops:
  6.5 91.0 %all-gather.7.cloned.1.call-start = ((), (), s32[]{:S(2)}) async-start(), calls=%async_computation.1 | async-start | bytes 9437184 | tf_op jit(solution)/shard_map/all_gather | solution.py:18
  7.8 18.2 %collective-permute-start = (s32[1]{0:T(128)}, s32[1]{0:T(128)}, u32[]{:S(2)}, u32[]{:S(2)}) collective-permute-start(s32[1]{0:T(128)} %bitcast.4), channel_id=1, source_target_pairs={{0,1},{1,2},{2,3},{3,4},{4,5},{5,6},{6,7},{8,9},{9,10},{10,11},{11... | collective-permute-start | bytes 20 | tf_op jit(solution)/shard_map/ppermute | solution.py:13
  18.1 7.9 %copy-start.3 = (s32[1,512]{1,0:T(1,128)S(1)}, s32[1,512]{1,0:T(1,128)}, u32[]{:S(2)}) copy-start(s32[1,512]{1,0:T(1,128)} %param.16) | copy-start | bytes 6148
  21.6 10.0 %copy-start.1 = (bf16[4,128,16,128]{1,3,2,0:T(8,128)(2,1)}, bf16[4,128,16,128]{1,3,2,0:T(8,128)(2,1)S(1)}, u32[]{:S(2)}) copy-start(bf16[4,128,16,128]{1,3,2,0:T(8,128)(2,1)S(1)} %copy.26) | copy-start | bytes 6291460
  41.6 1.0 copy-start
  42.6 154.5 %all-gather.5.cloned.1.call-start = ((), (), s32[]{:S(2)}) async-start(), calls=%async_computation | async-start | bytes 8650752 | tf_op jit(solution)/shard_map/all_gather | solution.py:100
  197.1 2.3 %copy-start.2 = (f32[4,128,16,128]{3,2,1,0:T(8,128)S(1)}, f32[4,128,16,128]{3,2,1,0:T(8,128)}, u32[]{:S(2)}) copy-start(f32[4,128,16,128]{3,2,1,0:T(8,128)} %copy.30) | copy-start | bytes 12582916
  197.1 2.9 %copy-start.4 = (bf16[1,512,2048]{2,1,0:T(8,128)(2,1)S(1)}, bf16[1,512,2048]{2,1,0:T(8,128)(2,1)}, u32[]{:S(2)}) copy-start(bf16[1,512,2048]{2,1,0:T(8,128)(2,1)} %param.15) | copy-start | bytes 6291460
  197.1 2.9 %copy-start.5 = (f32[2048]{0:T(1024)S(1)}, f32[2048]{0:T(1024)}, u32[]{:S(2)}) copy-start(f32[2048]{0:T(1024)} %param.18) | copy-start | bytes 24580
Sparse Core Ops, SparseCore 0:
  42.7 54.7 all-gather.6
  100.1 96.9 all-gather.4
where the time goes:
time: 220 us; the launch traced here: 219 us
  waiting for transfers between devices  106 us (48%)
  matrix products  30.9 us (14%)
  other arithmetic  28.8 us (13%)
  local copies, waits for them, and re-layouts  25.2 us (11%)
  between operations  13.6 us (6%)
  blocking collectives  9.47 us (4%)
  starting transfers between devices  4.53 us (2%)
    all_gather x1, waiting for transfers between devices, local(): lax.all_gather(w_out, 'pack', axis=0, tiled=True)  71.4 us
    all_gather x1, waiting for transfers between devices, carried_in(): everything = jax.tree.map(lambda part: lax.all_gather(part, axis), array)  34.2 us
    dot_general x1, matrix products, local(): jnp.dot(gated, lax.all_gather(w_out, 'pack', axis=0, tiled=True), preferr...  12.4 us
    select_n x8, other arithmetic, hop(): return jax.tree.map(lambda a, b: jnp.where(reached, a, b), new, before)  11.7 us
    unnamed x15, local copies, waits for them, and re-layouts  11.6 us
    all_gather x1, blocking collectives, carried_in(): everything = jax.tree.map(lambda part: lax.all_gather(part, axis), array)  9.47 us
    dot_general x1, matrix products, local(): jnp.einsum('nthd,nhde->nthe', q_blk, entering, preferred_element_type=jnp...  7.41 us
    dot_general x1, matrix products, local(): jnp.einsum('nhts,nshd->nthd', weights, v_blk, preferred_element_type=jnp....  6.81 us
  transfers between devices with their start and end apart: 3, of which 2 were waited for; matrix products, arithmetic and copies ran while one was open for 24% of the time, Pallas kernels for 0%

commit v1 on v0

--- a/solution.py
+++ b/solution.py
@@ -97,7 +97,11 @@
     normed = (centred * lax.rsqrt(variance + 1e-05)).reshape(length, width) * norm_gain
     gated = (jax.nn.silu(gates[0].astype(jnp.float32)) * normed).astype(jnp.bfloat16)
     mixed = jnp.dot(
-        gated, lax.all_gather(w_out, "pack", axis=0, tiled=True), preferred_element_type=jnp.float32
+        gated,
+        jnp.concatenate(
+            lax.all_to_all(jnp.stack([w_out] * lax.axis_size("pack")), "pack", 0, 0), axis=0
+        ),
+        preferred_element_type=jnp.float32,
     ).astype(jnp.bfloat16)
     return mixed[None]
 

time: 220 us -> 280 us (1.27)
  the two profiles are of different devices: /device:TPU:1 before, /device:TPU:107 now
where the time goes in v1:
time: 280 us; the launch traced here: 279 us
  waiting for transfers between devices  136 us (49%)
  local copies, waits for them, and re-layouts  46.8 us (17%)
  matrix products  31.9 us (11%)
  other arithmetic  28.8 us (10%)
  between operations  13.6 us (5%)
  starting transfers between devices  13.5 us (5%)
  blocking collectives  8.44 us (3%)
    all_to_all x1, waiting for transfers between devices, local(): lax.all_to_all(jnp.stack([w_out] * lax.axis_size('pack')), 'pack', 0, 0)  116 us
    all_gather x1, waiting for transfers between devices, carried_in(): everything = jax.tree.map(lambda part: lax.all_gather(part, axis), array)  19.6 us
    dot_general x1, matrix products, local(): jnp.dot(gated, jnp.concatenate(lax.all_to_all(jnp.stack([w_out] * lax.axi...  13.4 us
    select_n x8, other arithmetic, hop(): return jax.tree.map(lambda a, b: jnp.where(reached, a, b), new, before)  11.7 us
    unnamed x15, local copies, waits for them, and re-layouts  11.2 us
    all_to_all x1, starting transfers between devices, local(): lax.all_to_all(jnp.stack([w_out] * lax.axis_size('pack')), 'pack', 0, 0)  9.84 us
    all_gather x1, blocking collectives, carried_in(): everything = jax.tree.map(lambda part: lax.all_gather(part, axis), array)  8.44 us
    mul x2, local copies, waits for them, and re-layouts, local(): centred * lax.rsqrt(variance + 1e-05)  7.59 us
  transfers between devices with their start and end apart: 3, of which 2 were waited for; matrix products, arithmetic and copies ran while one was open for 27% of the time, Pallas kernels for 0%

profile of v1, /device:TPU:107, one launch (start us, length us, event | category | flops | bytes accessed | tf_op | source)
XLA Modules:
  0.0 278.9 jit_solution(6878262342603989463)
XLA Ops:
  6.5 1.3 slice.26
  7.8 3.7 %collective-permute-start = (s32[1]{0:T(128)}, s32[1]{0:T(128)}, u32[]{:S(2)}, u32[]{:S(2)}) collective-permute-start(s32[1]{0:T(128)} %bitcast.2), channel_id=1, source_target_pairs={{0,1},{1,2},{2,3},{3,4},{4,5},{5,6},{6,7},{8,9},{9,10},{10,11},{11... | collective-permute-start | bytes 20 | tf_op jit(solution)/shard_map/ppermute | solution.py:13
  11.5 0.9 slice_reduce_fusion
  12.4 0.7 multiply_exponential_fusion.3
  13.1 0.8 compare_convert_fusion.1
  13.8 3.5 %copy.41 = bf16[64,8,16,128]{3,2,1,0:T(8,128)(2,1)} copy(bf16[64,8,16,128]{3,1,2,0:T(8,128)(2,1)} %bitcast.79) | data formatting | bytes 4194304
  17.4 3.5 %copy.26 = bf16[4,128,16,128]{1,3,2,0:T(8,128)(2,1)S(1)} copy(bf16[4,128,16,128]{3,2,1,0:T(8,128)(2,1)} %bitcast.77) | data formatting | bytes 4194304 | tf_op jit(solution)/shard_map/reshape;squeeze | solution.py:52
  20.8 4.3 %copy.42 = bf16[64,8,16,128]{3,2,1,0:T(8,128)(2,1)} copy(bf16[64,8,16,128]{3,1,2,0:T(8,128)(2,1)} %bitcast.80) | data formatting | bytes 4194304
  25.2 0.8 fusion.30
  26.0 0.3 reduce_window_sum.11
  26.4 4.3 %fusion.9 = f32[4,16,128,128]{3,2,1,0:T(8,128)} fusion(bf16[4,128,16,128]{1,3,2,0:T(8,128)(2,1)S(1)} %copy.26, f32[4,128,16]{1,2,0:T(8,128)S(1)} %get-tuple-element.195, bf16[4,128,16,128]{3,2,1,0:T(8,128)(2,1)} %bitcast.75), kind=kOutput, calls=%fused_computation.22 | convolution fusion | flops 271581184 | bytes 8421376 | tf_op jit(solution)/shard_map/nshd,nshe->nhde/dot_general | solution.py:66
  30.8 10.1 %while.29 = (s32[]{:T(128)}, f32[16,128,128]{2,1,0:T(8,128)S(1)}, f32[4,16,128,128]{3,2,1,0:T(8,128)}, f32[4,16]{1,0:T(4,128)S(1)}, f32[4,16,128,128]{3,2,1,0:T(8,128)}) while((s32[]{:T(128)}, f32[16,128,128]{2,1,0:T(8,128)S(1)}, f32[4,16,128,128]{3,2,1,0:T(8,128)}, f32[4,16]{1,0:T(4,128)S(1)}, ...), condition=%wide.region_2.3_spmd.clone.clone, body=%wide.region_1.2_spmd.clone.sunk.clone | while | flops 1048579 | bytes 5243164 | solution.py:75
  30.8 1.1 bitcast_dynamic-update-slice_fusion.3
  31.9 1.4 bitcast_add_fusion.4
  33.3 1.0 bitcast_dynamic-update-slice_fusion.3
  34.4 1.4 bitcast_add_fusion.4
  35.8 1.1 bitcast_dynamic-update-slice_fusion.3
  36.9 1.4 bitcast_add_fusion.4
  38.4 1.1 bitcast_dynamic-update-slice_fusion.3
  39.4 1.4 bitcast_add_fusion.4
  40.9 1.0 copy-done
  41.9 4.3 %stack.2 = bf16[32,64,2048]{2,1,0:T(8,128)(2,1)} broadcast(bf16[64,2048]{1,0:T(8,128)(2,1)S(1)} %copy-done.2), dimensions={1,2} | broadcast | bytes 8650752 | tf_op jit(solution)/shard_map/stack | solution.py:102
  46.2 9.8 %all-to-all-start = ((bf16[32,64,2048]{2,1,0:T(8,128)(2,1)}), bf16[32,64,2048]{2,1,0:T(8,128)(2,1)}, u32[]{:S(2)}, u32[]{:S(2)}) async-start(bf16[32,64,2048]{2,1,0:T(8,128)(2,1)} %stack.2), calls=%async_computation | async-start | bytes 16777216 | tf_op jit(solution)/shard_map/all_to_all | solution.py:102
  56.0 2.4 copy.40
  58.4 0.1 compare_and_fusion
  58.6 1.2 multiply_exponential_fusion
  59.8 6.9 %fusion.16 = f32[4,16,128,128]{2,3,1,0:T(8,128)} fusion(bf16[4,128,16,128]{3,2,1,0:T(8,128)(2,1)} %bitcast.76, bf16[4,128,16,128]{1,3,2,0:T(8,128)(2,1)} %copy-done.1, f32[16,128,128]{2,1,0:T(8,128)} %multiply_exponential_fusion, pred[4,128,128]{2,1,0:T(8,128)(4,1)S(1)} %compare_and_fusion, bf16[4,128,16,128]{3,2,1,0:T(8,128)(2,1)S(1)} %bitcast.73), kind=kOutput, calls=%fused_computation.28 | convolution fusion | flops 540016640 | bytes 11599872 | tf_op jit(solution)/shard_map/nhts,nshd->nthd/dot_general | solution.py:62
  66.7 8.4 %all-gather.1 = f32[8,1,16]{2,1,0:T(1,128)S(1)} all-gather(f32[1,1,16]{2,1,0:T(1,128)S(1)} %multiply_bitcast_fusion), channel_id=1, replica_groups=mesh['pack'=32,'hist'=8] {'hist'}, dimensions={0}, use_global_device_ids=true | all-gather | bytes 576 | tf_op jit(solution)/shard_map/all_gather | solution.py:18
  75.2 19.6 %all-gather.4.cloned.1.call-done = f32[128,128,128]{2,1,0:T(8,128)} async-done(((f32[16,128,128]{2,1,0:T(8,128)}), f32[128,128,128]{2,1,0:T(8,128)}) %all-gather.4.cloned.1.call-update) | async-done | bytes 8388624 | tf_op jit(solution)/shard_map/all_gather | solution.py:18
  94.8 12.0 %while.30 = (s32[]{:T(128)}, f32[16,128,128]{2,1,0:T(8,128)S(1)}, s32[]{:T(128)}, f32[8,16]{1,0:T(8,128)S(1)}, f32[8,16,128,128]{3,2,1,0:T(8,128)}) while((s32[]{:T(128)}, f32[16,128,128]{2,1,0:T(8,128)S(1)}, s32[]{:T(128)}, f32[8,16]{1,0:T(8,128)S(1)}, f32[8,16,128,128]{3,2,1,0:T(8,128)}) %tuple.69), condition=%wide.region_5.6_spmd.clone.clone, body=%wide.region_4.5_spmd.clone.sunk.clone | while | flops 1048580 | bytes 3146017 | solution.py:30
  94.8 1.5 fusion.40
  96.3 1.5 fusion.40
  97.8 1.5 fusion.40
  99.3 1.5 fusion.40
  100.8 1.5 fusion.40
  102.3 1.5 fusion.40
  103.8 1.5 fusion.40
  105.3 1.5 fusion.40
  106.8 7.3 %fusion.32 = (f32[4,128,16]{1,2,0:T(8,128)S(1)}, f32[4,128,16,128]{1,3,2,0:T(8,128)}) fusion(f32[4,128,16]{1,2,0:T(8,128)S(1)} %get-tuple-element.194, bf16[4,128,16,128]{3,2,1,0:T(8,128)(2,1)S(1)} %bitcast.74, f32[4,16,128,128]{3,2,1,0:T(8,128)} %get-tuple-element.127, f32[16,128,128]{2,1,0:T(8,128)S(1)} %get-tuple-element.129, ...), kind=kOutput, calls=%fused_computation.63 | convolution fusion | flops 274718720 | bytes 15794432 | tf_op jit(solution)/shard_map/nthd,nhde->nthe/dot_general | solution.py:90
  114.1 5.4 %copy.30 = f32[4,128,16,128]{3,2,1,0:T(8,128)} copy(f32[4,128,16,128]{1,3,2,0:T(8,128)} %get-tuple-element.193) | data formatting | bytes 8388608 | tf_op jit(solution)/shard_map/add | solution.py:93
  119.5 4.9 %reshape.270 = f32[1,512,2048]{2,1,0:T(8,128)} reshape(f32[4,128,16,128]{3,2,1,0:T(8,128)} %copy.30) | data formatting | bytes 8388608 | tf_op jit(solution)/shard_map/reshape | solution.py:93
  124.5 3.0 %multiply_reduce_fusion = f32[4,128,16]{1,2,0:T(8,128)S(1)} fusion(f32[4,128,16,128]{1,3,2,0:T(8,128)} %get-tuple-element.193, f32[4,128,16]{1,2,0:T(8,128)S(1)} %broadcast_multiply_fusion), kind=kLoop, calls=%fused_computation.15 | loop fusion | flops 3137536 | bytes 4259840 | tf_op jit(solution)/shard_map/reduce_sum | solution.py:96
  127.7 2.6 sub.64
  130.3 4.9 %sub.65 = f32[1,512,2048]{2,1,0:T(8,128)} reshape(f32[512,16,128]{2,1,0:T(8,128)} %sub.64) | data formatting | bytes 8388608 | tf_op jit(solution)/shard_map/sub | solution.py:95
  135.2 2.6 mul.237
  137.7 5.0 %mul.238 = f32[1,512,2048]{2,1,0:T(8,128)} reshape(f32[512,16,128]{2,1,0:T(8,128)} %mul.237) | data formatting | bytes 8388608 | tf_op jit(solution)/shard_map/mul | solution.py:97
  142.8 115.9 %all-to-all-done = bf16[32,64,2048]{2,1,0:T(8,128)(2,1)} async-done(((bf16[32,64,2048]{2,1,0:T(8,128)(2,1)}), bf16[32,64,2048]{2,1,0:T(8,128)(2,1)}, u32[]{:S(2)}, u32[]{:S(2)}) %all-to-all-start) | async-done | bytes 8388640 | tf_op jit(solution)/shard_map/all_to_all | solution.py:102
  258.7 13.4 %fusion.8 = bf16[1,512,2048]{2,1,0:T(8,128)(2,1)} fusion(bf16[2048,2048]{1,0:T(8,128)(2,1)} %bitcast.12, f32[1,512,2048]{2,1,0:T(8,128)} %mul.238, f32[1,512,2048]{2,1,0:T(8,128)} %reshape.270, f32[1,512,2048]{2,1,0:T(8,128)} %sub.65, bf16[1,512,2048]{2,1,0:T(8,128)(2,1)S(1)} %copy-done.4, f32[2048]{0:T(1024)S(1)} %copy-done.5), kind=kOutput, calls=%fused_computation.21 | convolution fusion | flops 4306501632 | bytes 25174016 | tf_op jit(solution)/shard_map/dot_general | solution.py:99
  (44 shorter events, 0.7 us)
Async XLA Ops:
  6.5 88.3 %all-gather.4.cloned.1.call-start = ((), (), s32[]{:S(2)}) async-start(), calls=%async_computation.1 | async-start | bytes 9437184 | tf_op jit(solution)/shard_map/all_gather | solution.py:18
  7.8 17.4 %collective-permute-start = (s32[1]{0:T(128)}, s32[1]{0:T(128)}, u32[]{:S(2)}, u32[]{:S(2)}) collective-permute-start(s32[1]{0:T(128)} %bitcast.2), channel_id=1, source_target_pairs={{0,1},{1,2},{2,3},{3,4},{4,5},{5,6},{6,7},{8,9},{9,10},{10,11},{11... | collective-permute-start | bytes 20 | tf_op jit(solution)/shard_map/ppermute | solution.py:13
  17.4 7.9 %copy-start.3 = (s32[1,512]{1,0:T(1,128)S(1)}, s32[1,512]{1,0:T(1,128)}, u32[]{:S(2)}) copy-start(s32[1,512]{1,0:T(1,128)} %param.16) | copy-start | bytes 6148
  20.8 9.9 %copy-start.1 = (bf16[4,128,16,128]{1,3,2,0:T(8,128)(2,1)}, bf16[4,128,16,128]{1,3,2,0:T(8,128)(2,1)S(1)}, u32[]{:S(2)}) copy-start(bf16[4,128,16,128]{1,3,2,0:T(8,128)(2,1)S(1)} %copy.26) | copy-start | bytes 6291460
  30.8 11.1 %copy-start.2 = (bf16[64,2048]{1,0:T(8,128)(2,1)S(1)}, bf16[64,2048]{1,0:T(8,128)(2,1)}, u32[]{:S(2)}) copy-start(bf16[64,2048]{1,0:T(8,128)(2,1)} %param.19) | copy-start | bytes 786436
  40.9 1.0 copy-start
  46.2 212.5 %all-to-all-start = ((bf16[32,64,2048]{2,1,0:T(8,128)(2,1)}), bf16[32,64,2048]{2,1,0:T(8,128)(2,1)}, u32[]{:S(2)}, u32[]{:S(2)}) async-start(bf16[32,64,2048]{2,1,0:T(8,128)(2,1)} %stack.2), calls=%async_computation | async-start | bytes 16777216 | tf_op jit(solution)/shard_map/all_to_all | solution.py:102
  137.7 120.9 %copy-start.4 = (bf16[1,512,2048]{2,1,0:T(8,128)(2,1)S(1)}, bf16[1,512,2048]{2,1,0:T(8,128)(2,1)}, u32[]{:S(2)}) copy-start(bf16[1,512,2048]{2,1,0:T(8,128)(2,1)} %param.15) | copy-start | bytes 6291460
  137.7 120.9 %copy-start.5 = (f32[2048]{0:T(1024)S(1)}, f32[2048]{0:T(1024)}, u32[]{:S(2)}) copy-start(f32[2048]{0:T(1024)} %param.18) | copy-start | bytes 24580
Sparse Core Ops, SparseCore 0:
  42.0 52.7 all-gather.3
